TPU v7x, 256 devices: a whole 4x4x8 slice. The times are simulated.
256 devices in a mesh: shard: 16 (over y, z_hi, core), rep: 16 (over x, z_lo).
Axes of the slice: x: 4, y: 4, z: 8 (z_hi: 2, z_lo: 4; z = z_hi * 4 + z_lo), core: 2. Of those that a mesh axis runs over, the one named last changes fastest.
Arguments:
- inputs: bfloat16 [50432, 768], P(('shard', 'rep')), may hold values from -6 to 6
- norm1_gain: float32 [768], replicated, may hold values from 0.25 to 1.75
- w_qkv: bfloat16 [768, 2304], P('shard'), may hold values from -0.21875 to 0.21875
- w_proj: bfloat16 [768, 768], P('shard'), may hold values from -0.875 to 0.875
- norm2_gain: float32 [768], replicated, may hold values from 0.25 to 1.75
- w_router: bfloat16 [768, 32], P('shard'), may hold values from -0.21875 to 0.21875
- w_expert_in: bfloat16 [2, 768, 3072], P(None, 'shard'), may hold values from -0.21875 to 0.21875
- w_expert_out: bfloat16 [2, 3072, 768], P(None, 'shard'), may hold values from -0.875 to 0.875
- expert_ids: int32 [50432, 2], P(('shard', 'rep')), may hold values from 0 to 1, all different within a row
- capacity: int32 [2], replicated, may hold values from 64 to 128, as said below
- cotangent: bfloat16 [50432, 768], P(('shard', 'rep')), may hold values from -6 to 6
Outputs:
- outputs: bfloat16 [50432, 768], P(('shard', 'rep'))
- grad_inputs: float32 [50432, 768], P(('shard', 'rep'))
- grad_norm1_gain: float32 [768], replicated
- grad_qkv: float32 [768, 2304], P('shard')
- grad_proj: float32 [768, 768], P('shard')
- grad_norm2_gain: float32 [768], replicated
- grad_router: float32 [768, 32], P('shard')
- grad_expert_in: float32 [2, 768, 3072], P(None, 'shard')
- grad_expert_out: float32 [2, 3072, 768], P(None, 'shard')
Inputs may be any that keep to these rules, and one draw needn't show every extreme that they name: Every expert's capacity is 64 to 128; some expert has exactly 128. `expert_ids`: the two experts of a token differ.
All inputs are finite; a program needn't handle non-finite values.
Results may differ from a plain program's by a relative error of at most 0.025.
Values may be sent and summed in bfloat16 or wider, within the bound.
No kernel may reach another device: no remote copies, remote signals or barrier semaphores. Data moves between devices by JAX's collectives and lax.ppermute only.
A program may use at most 128 MiB of HBM per device.

v0:
```python
import jax
import jax.numpy as jnp
from jax import lax
from jax.sharding import PartitionSpec as P

HEADS = 12
HD = 64
EXPERTS = 32
E_WIN = 2
SEQ = 197
CAP = 128
EPS = 1e-06


def layer_norm(values, gain):
    centred = values - jnp.mean(values, axis=-1, keepdims=True)
    inverse = lax.rsqrt(jnp.mean(centred * centred, axis=-1, keepdims=True) + EPS)
    normed = centred * inverse
    return (normed, inverse, (normed * gain).astype(jnp.bfloat16))


def layer_norm_back(grad_out, normed, inverse, gain):
    scaled = grad_out * gain
    grad_in = inverse * (
        scaled
        - jnp.mean(scaled, axis=-1, keepdims=True)
        - normed * jnp.mean(scaled * normed, axis=-1, keepdims=True)
    )
    return (grad_in, jnp.sum(grad_out * normed, axis=0))


def heads_view(block, images):
    return block.reshape(images, SEQ, HEADS, HD)


def attention_scores(qkv, images):
    width = HEADS * HD
    query = heads_view(qkv[:, :width], images)
    keys = heads_view(qkv[:, width : 2 * width], images)
    values = heads_view(qkv[:, 2 * width :], images)
    scores = jnp.einsum(
        "bqhd,bkhd->bhqk", query, keys, preferred_element_type=jnp.float32
    ) * HD ** (-0.5)
    return (query, keys, values, scores)


def attention_forward(qkv, images):
    query, keys, values, scores = attention_scores(qkv, images)
    logsum = jax.nn.logsumexp(scores, axis=-1, keepdims=True)
    probs = jnp.exp(scores - logsum).astype(jnp.bfloat16)
    mixed = jnp.einsum("bhqk,bkhd->bqhd", probs, values, preferred_element_type=jnp.float32).astype(
        jnp.bfloat16
    )
    return (mixed.reshape(images * SEQ, HEADS * HD), logsum)


def attention_backward(qkv, mixed, logsum, grad_mixed, images):
    query, keys, values, scores = attention_scores(qkv, images)
    probs_full = jnp.exp(scores - logsum)
    probs = probs_full.astype(jnp.bfloat16)
    grad_out = heads_view(grad_mixed, images)
    out_rows = heads_view(mixed, images)
    grad_values = jnp.einsum("bhqk,bqhd->bkhd", probs, grad_out, preferred_element_type=jnp.float32)
    grad_probs = jnp.einsum("bqhd,bkhd->bhqk", grad_out, values, preferred_element_type=jnp.float32)
    delta = jnp.sum(grad_out.astype(jnp.float32) * out_rows.astype(jnp.float32), axis=-1)
    delta = jnp.transpose(delta, (0, 2, 1))[..., None]
    grad_scores = (probs_full * (grad_probs - delta)).astype(jnp.bfloat16)
    scale = HD ** (-0.5)
    grad_query = (
        jnp.einsum("bhqk,bkhd->bqhd", grad_scores, keys, preferred_element_type=jnp.float32) * scale
    )
    grad_keys = (
        jnp.einsum("bhqk,bqhd->bkhd", grad_scores, query, preferred_element_type=jnp.float32)
        * scale
    )
    width = HEADS * HD
    rows = images * SEQ
    return jnp.concatenate(
        [
            grad_query.reshape(rows, width),
            grad_keys.reshape(rows, width),
            grad_values.reshape(rows, width),
        ],
        axis=1,
    ).astype(jnp.bfloat16)


def route_masks(expert_ids, capacity):
    count = expert_ids.shape[0]
    picked_hot = (expert_ids[:, :, None] == jnp.arange(E_WIN)[None, None, :]).astype(jnp.int32)
    ordered = jnp.transpose(picked_hot, (1, 0, 2)).reshape(2 * count, E_WIN)
    before = jnp.cumsum(ordered, axis=0) - ordered
    position = jnp.sum(before * ordered, axis=1).reshape(2, count).T
    limit = jnp.sum(picked_hot * capacity[None, None, :], axis=2)
    kept_mask = (position < limit).astype(jnp.float32)
    slot_hot = (position[:, :, None] == jnp.arange(CAP)[None, None, :]).astype(jnp.float32)
    return (
        kept_mask[:, :, None, None]
        * picked_hot.astype(jnp.float32)[:, :, :, None]
        * slot_hot[:, :, None, :]
    )


def body(
    inputs,
    norm1_gain,
    w_qkv,
    w_proj,
    norm2_gain,
    w_router,
    w_expert_in,
    w_expert_out,
    expert_ids,
    capacity,
    cotangent,
):
    high = lax.Precision.HIGHEST
    images = inputs.shape[0] // SEQ
    shard_rows = w_qkv.shape[0]
    hid_rows = w_expert_out.shape[1]
    full_qkv, full_proj, full_router = (
        lax.all_gather(w_qkv, "shard", axis=0, tiled=True),
        lax.all_gather(w_proj, "shard", axis=0, tiled=True),
        lax.all_gather(w_router, "shard", axis=0, tiled=True),
    )
    x_float = inputs.astype(jnp.float32)
    normed1, inverse1, hidden1 = layer_norm(x_float, norm1_gain)
    qkv = jnp.dot(hidden1, full_qkv, preferred_element_type=jnp.float32).astype(jnp.bfloat16)
    mixed, logsum = attention_forward(qkv, images)
    attended = x_float + jnp.dot(mixed, full_proj, preferred_element_type=jnp.float32)
    normed2, inverse2, hidden2 = layer_norm(attended, norm2_gain)
    logits = jnp.dot(hidden2, full_router, preferred_element_type=jnp.float32)
    router = jax.nn.softmax(logits, axis=-1)
    expert_hot = (expert_ids[:, :, None] == jnp.arange(EXPERTS)[None, None, :]).astype(jnp.float32)
    gate = jnp.sum(router[:, None, :] * expert_hot, axis=2)
    masks = route_masks(expert_ids, capacity)
    dispatch_float = jnp.sum(masks, axis=1)
    dispatch = dispatch_float.astype(jnp.bfloat16)
    combine = jnp.sum(masks * gate[:, :, None, None], axis=1)
    expert_rows = jnp.einsum(
        "rec,rd->ecd", dispatch, hidden2, preferred_element_type=jnp.float32
    ).astype(jnp.bfloat16)
    kept_weights = []
    pre_list = []
    activated_list = []
    eout_list = []
    for expert in range(E_WIN):
        first, second = (
            lax.all_gather(w_expert_in[expert], "shard", axis=0, tiled=True),
            lax.all_gather(w_expert_out[expert], "shard", axis=0, tiled=True),
        )
        kept_weights.append((first, second))
        pre = jnp.dot(expert_rows[expert], first, preferred_element_type=jnp.float32)
        activated = jax.nn.gelu(pre, approximate=False).astype(jnp.bfloat16)
        pre_list.append(pre)
        activated_list.append(activated)
        eout_list.append(
            jnp.dot(activated, second, preferred_element_type=jnp.float32).astype(jnp.bfloat16)
        )
    expert_out = jnp.stack(eout_list)
    eout_float = expert_out.astype(jnp.float32)
    moe = jnp.einsum("rec,ecd->rd", combine, eout_float, precision=high)
    outputs = (attended + moe).astype(jnp.bfloat16)
    grad = cotangent.astype(jnp.float32)
    matched = jnp.einsum("rd,ecd->rec", grad, eout_float, precision=high)
    grad_gate = jnp.sum(masks * matched[:, None, :, :], axis=(2, 3))
    grad_eout = jnp.einsum("rec,rd->ecd", combine, grad, precision=high).astype(jnp.bfloat16)
    back_qkv, back_proj, back_router = (full_qkv, full_proj, full_router)
    in_list = []
    out_list = []
    grad_rows_list = []
    for expert in range(E_WIN):
        first, second = kept_weights[expert]
        pre = pre_list[expert]
        grad_act = jnp.einsum(
            "cd,hd->ch", grad_eout[expert], second, preferred_element_type=jnp.float32
        )
        slope = (
            0.5 * (1.0 + jax.scipy.special.erf(pre * 0.7071067811865476))
            + pre * jnp.exp(-0.5 * pre * pre) * 0.3989422804014327
        )
        grad_pre = (grad_act * slope).astype(jnp.bfloat16)
        grad_rows_list.append(
            jnp.einsum("ch,dh->cd", grad_pre, first, preferred_element_type=jnp.float32).astype(
                jnp.bfloat16
            )
        )
        rows_here = expert_rows[expert]
        act_here = activated_list[expert]
        eout_here = grad_eout[expert]

        def in_term(start, count, rows_here=rows_here, grad_pre=grad_pre):
            return jnp.einsum("cd,ch->dh", rows_here, grad_pre, preferred_element_type=jnp.float32)

        def out_term(start, count, act_here=act_here, eout_here=eout_here):
            return jnp.einsum("ch,cd->hd", act_here, eout_here, preferred_element_type=jnp.float32)

        in_list.append(
            lax.psum_scatter(
                in_term(jnp.int32(0), shard_rows * lax.axis_size("shard")).astype(jnp.bfloat16),
                "shard",
                scatter_dimension=0,
                tiled=True,
            ).astype(jnp.float32)
        )
        out_list.append(
            lax.psum_scatter(
                out_term(jnp.int32(0), hid_rows * lax.axis_size("shard")).astype(jnp.bfloat16),
                "shard",
                scatter_dimension=0,
                tiled=True,
            ).astype(jnp.float32)
        )
    grad_rows = jnp.stack(grad_rows_list)
    grad_probs = jnp.sum(grad_gate[:, :, None] * expert_hot, axis=1)
    grad_logits = (
        router * (grad_probs - jnp.sum(router * grad_probs, axis=-1, keepdims=True))
    ).astype(jnp.bfloat16)
    grad_hidden2 = jnp.einsum(
        "rec,ecd->rd", dispatch, grad_rows, preferred_element_type=jnp.float32
    ) + jnp.einsum("re,de->rd", grad_logits, back_router, preferred_element_type=jnp.float32)
    grad_norm2, gain2 = layer_norm_back(grad_hidden2, normed2, inverse2, norm2_gain)
    grad_attended = grad + grad_norm2
    grad_branch = grad_attended.astype(jnp.bfloat16)
    grad_mixed = jnp.einsum(
        "rk,dk->rd", grad_branch, back_proj, preferred_element_type=jnp.float32
    ).astype(jnp.bfloat16)
    grad_qkv_rows = attention_backward(qkv, mixed, logsum, grad_mixed, images)
    grad_hidden1 = jnp.einsum(
        "rk,dk->rd", grad_qkv_rows, back_qkv, preferred_element_type=jnp.float32
    )
    grad_norm1, gain1 = layer_norm_back(grad_hidden1, normed1, inverse1, norm1_gain)
    grad_inputs = grad_attended + grad_norm1
    gain1_total, gain2_total = lax.psum((gain1, gain2), ("shard", "rep"))
    dense_local = lax.psum_scatter(
        jnp.concatenate(
            [
                jnp.einsum("rc,rk->ck", hidden1, grad_qkv_rows, preferred_element_type=jnp.float32),
                jnp.einsum("rc,rk->ck", mixed, grad_branch, preferred_element_type=jnp.float32),
                jnp.einsum("rc,rk->ck", hidden2, grad_logits, preferred_element_type=jnp.float32),
            ],
            axis=1,
        ).astype(jnp.bfloat16),
        "shard",
        scatter_dimension=0,
        tiled=True,
    )
    dense_total, in_total, out_total = (
        lax.psum(dense_local, "rep").astype(jnp.float32),
        lax.psum(jnp.stack(in_list).astype(jnp.bfloat16), "rep").astype(jnp.float32),
        lax.psum(jnp.stack(out_list).astype(jnp.bfloat16), "rep").astype(jnp.float32),
    )
    width = HEADS * HD
    return (
        outputs,
        grad_inputs,
        gain1_total,
        dense_total[:, : 3 * width],
        dense_total[:, 3 * width : 4 * width],
        gain2_total,
        dense_total[:, 4 * width :],
        in_total,
        out_total,
    )


def solution(mesh):
    in_specs = (
        P(("shard", "rep"), None),
        P(),
        P("shard", None),
        P("shard", None),
        P(),
        P("shard", None),
        P(None, "shard", None),
        P(None, "shard", None),
        P(("shard", "rep"), None),
        P(),
        P(("shard", "rep"), None),
    )
    out_specs = (
        P(("shard", "rep"), None),
        P(("shard", "rep"), None),
        P(),
        P("shard", None),
        P("shard", None),
        P(),
        P("shard", None),
        P(None, "shard", None),
        P(None, "shard", None),
    )
    return jax.shard_map(body, mesh=mesh, in_specs=in_specs, out_specs=out_specs, check_vma=False)
```

profile of v0, /device:TPU:24, one launch (start us, length us, event | category | flops | bytes accessed | tf_op | source)
XLA Modules:
  0.0 1204.1 jit_solution(413905897846838815)
XLA Ops:
  8.0 0.7 all-gather.14.cloned.1.call-update
  8.7 1.9 fusion.130
  10.7 0.9 fusion.129
  14.3 31.0 %all-gather.4 = bf16[16,48,32]{1,2,0:T(8,128)(2,1)S(1)} all-gather(bf16[1,48,32]{1,2,0:T(8,128)(2,1)S(1)} %bitcast.199), channel_id=1, replica_groups=mesh['shard'=16,'rep'=16] {'shard'}, dimensions={0}, use_global_device_ids=true | all-gather | bytes 52224 | tf_op jit(solution)/shard_map/all_gather | solution.py:124
  45.4 0.8 reshape.247
  47.8 39.1 %all-gather.12.cloned.1.call-done = bf16[768,2304]{1,0:T(8,128)(2,1)} async-done(((bf16[48,2304]{1,0:T(8,128)(2,1)}), bf16[768,2304]{1,0:T(8,128)(2,1)}) %all-gather.12.cloned.1.call-update) | async-done | bytes 3538960 | tf_op jit(solution)/shard_map/all_gather | solution.py:122
  86.8 3.0 convolution_convert_fusion.5
  89.9 0.9 copy.108
  90.8 0.9 copy.107
  91.9 1.8 multiply_reduce_fusion
  94.3 1.4 convolution_convert_fusion.10
  95.6 46.1 %all-gather.14.cloned.1.call-done = bf16[768,768]{1,0:T(8,128)(2,1)} async-done(((bf16[48,768]{1,0:T(8,128)(2,1)}), bf16[768,768]{1,0:T(8,128)(2,1)}) %all-gather.14.cloned.1.call-update) | async-done | bytes 1179664 | tf_op jit(solution)/shard_map/all_gather | solution.py:123
  141.7 1.9 fusion.131
  144.6 0.7 copy-done.6
  146.3 1.4 copy.113
  147.7 2.0 convolution_convert_fusion.9
  149.7 72.3 %all-gather.20.cloned.1.call-done = bf16[1,768,3072]{2,1,0:T(8,128)(2,1)} async-done(((bf16[1,48,3072]{2,1,0:T(8,128)(2,1)}), bf16[1,768,3072]{2,1,0:T(8,128)(2,1)}) %all-gather.20.cloned.1.call-update) | async-done | bytes 4718608 | tf_op jit(solution)/shard_map/all_gather | solution.py:149
  222.0 7.7 fusion.34
  229.7 71.5 %all-gather.22.cloned.1.call-done = bf16[1,3072,768]{2,1,0:T(8,128)(2,1)} async-done(((bf16[1,192,768]{2,1,0:T(8,128)(2,1)}), bf16[1,3072,768]{2,1,0:T(8,128)(2,1)}) %all-gather.22.cloned.1.call-update) | async-done | bytes 4718608 | tf_op jit(solution)/shard_map/all_gather | solution.py:150
  301.2 4.0 fusion.73
  305.2 75.7 %all-gather.16.cloned.1.call-done = bf16[1,768,3072]{2,1,0:T(8,128)(2,1)} async-done(((bf16[1,48,3072]{2,1,0:T(8,128)(2,1)}), bf16[1,768,3072]{2,1,0:T(8,128)(2,1)}) %all-gather.16.cloned.1.call-update) | async-done | bytes 4718608 | tf_op jit(solution)/shard_map/all_gather | solution.py:149
  380.9 7.9 fusion.31
  388.8 71.3 %all-gather.18.cloned.1.call-done = bf16[1,3072,768]{2,1,0:T(8,128)(2,1)} async-done(((bf16[1,192,768]{2,1,0:T(8,128)(2,1)}), bf16[1,3072,768]{2,1,0:T(8,128)(2,1)}) %all-gather.18.cloned.1.call-update) | async-done | bytes 4718608 | tf_op jit(solution)/shard_map/all_gather | solution.py:150
  460.1 3.4 fusion.79
  464.7 7.0 fusion.100
  472.9 0.7 copy-done.23
  473.7 3.7 convolution_convert_fusion
  477.4 4.7 convolution_convert_fusion.1
  482.3 4.8 fusion.22
  487.1 0.9 copy-done.12
  488.0 3.7 convolution_convert_fusion.2
  491.9 5.0 fusion.25
  496.9 0.9 copy-done.14
  497.8 3.5 convolution_convert_fusion.3
  501.4 1.6 copy.119
  503.7 4.3 fusion.82
  508.1 4.1 fusion.76
  513.4 0.8 copy-done
  514.2 1.3 convolution_convert_fusion.11
  515.5 1.9 copy.120
  517.4 2.0 copy.121
  519.4 1.1 convolution_convert_fusion.12
  520.6 0.8 copy.127
  521.4 1.4 multiply_reduce_fusion.1
  522.8 1.9 multiply_convert_fusion
  527.9 1.3 convolution_convert_fusion.4
  529.2 2.4 pad_maximum_fusion
  531.7 49.8 %reduce-scatter.14.cloned.1.call-done = bf16[192,768]{1,0:T(8,128)(2,1)} async-done(((bf16[3072,768]{1,0:T(8,128)(2,1)}), bf16[192,768]{1,0:T(8,128)(2,1)}) %reduce-scatter.14.cloned.1.call-update) | async-done | bytes 294928 | tf_op jit(solution)/shard_map/reduce_scatter | solution.py:207
  581.5 109.2 %reduce-scatter.12.cloned.1.call-done = bf16[192,768]{1,0:T(8,128)(2,1)} async-done(((bf16[3072,768]{1,0:T(8,128)(2,1)}), bf16[192,768]{1,0:T(8,128)(2,1)}) %reduce-scatter.12.cloned.1.call-update) | async-done | bytes 294928 | tf_op jit(solution)/shard_map/reduce_scatter | solution.py:207
  690.7 1.9 pad_maximum_fusion.3
  692.6 106.6 %reduce-scatter.10.cloned.1.call-done = bf16[48,3072]{1,0:T(8,128)(2,1)} async-done(((bf16[768,3072]{1,0:T(8,128)(2,1)}), bf16[48,3072]{1,0:T(8,128)(2,1)}) %reduce-scatter.10.cloned.1.call-update) | async-done | bytes 294928 | tf_op jit(solution)/shard_map/reduce_scatter | solution.py:199
  799.3 109.0 %reduce-scatter.8.cloned.1.call-done = bf16[48,3072]{1,0:T(8,128)(2,1)} async-done(((bf16[768,3072]{1,0:T(8,128)(2,1)}), bf16[48,3072]{1,0:T(8,128)(2,1)}) %reduce-scatter.8.cloned.1.call-update) | async-done | bytes 294928 | tf_op jit(solution)/shard_map/reduce_scatter | solution.py:199
  908.3 1.9 pad_maximum_fusion.2
  910.2 108.5 %reduce-scatter.6.cloned.1.call-done = bf16[48,3104]{1,0:T(8,128)(2,1)} async-done(((bf16[768,3104]{1,0:T(8,128)(2,1)}), bf16[48,3104]{1,0:T(8,128)(2,1)}) %reduce-scatter.6.cloned.1.call-update) | async-done | bytes 298000 | tf_op jit(solution)/shard_map/reduce_scatter | solution.py:235
  1018.8 4.2 fusion.96
  1022.9 74.5 %all-reduce.1 = (f32[768]{0:T(1024)}, f32[768]{0:T(1024)}) all-reduce(f32[768]{0:T(1024)S(1)} %get-tuple-element.56, f32[768]{0:T(1024)S(1)} %get-tuple-element.54), channel_id=1, replica_groups=mesh['shard'=16,'rep'=16] {'shard','rep'}, use_global_device_ids=true, to_apply=%region_24.25 | all-reduce | flops 1536 | bytes 12288 | tf_op jit(solution)/shard_map/psum | solution.py:234
  1098.8 1.1 fusion.60
  1100.0 1.1 fusion.95
  1101.1 88.9 %all-reduce.5.cloned.1.call-done = (bf16[48,3104]{1,0:T(8,128)(2,1)}, bf16[2,48,3072]{2,1,0:T(8,128)(2,1)}, bf16[2,192,768]{2,1,0:T(8,128)(2,1)}) async-done(((bf16[48,3104]{1,0:T(8,128)(2,1)}, bf16[2,48,3072]{2,1,0:T(8,128)(2,1)}, bf16[2,192,768]{2,1,0:T(8,128)(2,1)}), (bf16[48,3104]{1,0:T(8,128)(2,1)}, bf16[2,48,3072]{2,1,0:T(8,128)(2,1)}, bf16[2,192,768]{2,1,0:T(8,128)(2,1)})) %all-reduce.5.cloned.1.call-update) | async-done | bytes 1477648 | tf_op jit(solution)/shard_map/psum | solution.py:249
  1189.9 0.8 slice.86
  1190.7 1.6 slice.85
  1192.3 1.7 slice.84
  1194.7 1.1 convert_element_type.191
  1195.8 1.1 convert_element_type.194
  (179 shorter events, 17.6 us)
Async XLA Ops:
  7.2 3.5 copy-start.33
  7.2 79.7 %all-gather.12.cloned.1.call-start = ((), (), s32[]{:S(2)}) async-start(), calls=%async_computation.5 | async-start | bytes 3760128 | tf_op jit(solution)/shard_map/all_gather | solution.py:122
  7.9 133.8 %all-gather.14.cloned.1.call-start = ((), (), s32[]{:S(2)}) async-start(), calls=%async_computation.6 | async-start | bytes 1253376 | tf_op jit(solution)/shard_map/all_gather | solution.py:123
  8.7 4.2 copy-start.43
  8.7 213.3 %all-gather.20.cloned.1.call-start = ((), (), s32[]{:S(2)}) async-start(), calls=%async_computation.14 | async-start | bytes 5013504 | tf_op jit(solution)/shard_map/all_gather | solution.py:149
  10.6 3.7 copy-start.52
  10.6 35.6 %copy-start.53 = (s32[2]{0:T(128)S(1)}, s32[2]{0:T(128)}, u32[]{:S(2)}) copy-start(s32[2]{0:T(128)} %param.20) | copy-start | bytes 28
  10.7 35.8 %copy-start.3 = (bf16[197,768]{1,0:T(8,128)(2,1)S(1)}, bf16[197,768]{1,0:T(8,128)(2,1)}, u32[]{:S(2)}) copy-start(bf16[197,768]{1,0:T(8,128)(2,1)} %param.11) | copy-start | bytes 907780
  10.7 290.5 %all-gather.22.cloned.1.call-start = ((), (), s32[]{:S(2)}) async-start(), calls=%async_computation.15 | async-start | bytes 5013504 | tf_op jit(solution)/shard_map/all_gather | solution.py:150
  11.6 75.2 %copy-start.45 = (f32[768]{0:T(1024)S(1)}, f32[768]{0:T(1024)}, u32[]{:S(2)}) copy-start(f32[768]{0:T(1024)} %param.12) | copy-start | bytes 9220
  11.6 369.3 %all-gather.16.cloned.1.call-start = ((), (), s32[]{:S(2)}) async-start(), calls=%async_computation.12 | async-start | bytes 5013504 | tf_op jit(solution)/shard_map/all_gather | solution.py:149
  12.2 447.9 %all-gather.18.cloned.1.call-start = ((), (), s32[]{:S(2)}) async-start(), calls=%async_computation.13 | async-start | bytes 5013504 | tf_op jit(solution)/shard_map/all_gather | solution.py:150
  12.8 568.7 %reduce-scatter.14.cloned.1.call-start = ((), (), s32[]{:S(2)}) async-start(), calls=%async_computation.11 | async-start | bytes 5013504 | tf_op jit(solution)/shard_map/reduce_scatter | solution.py:207
  46.5 43.3 %copy-start.19 = (f32[197,2,2]{2,1,0:T(2,128)}, f32[197,2,2]{2,1,0:T(2,128)S(1)}, u32[]{:S(2)}) copy-start(f32[197,2,2]{2,1,0:T(2,128)S(1)} %copy.110) | copy-start | bytes 9460
  46.6 43.2 %copy-start.46 = (f32[197]{0:T(256)}, f32[197]{0:T(256)S(1)}, u32[]{:S(2)}) copy-start(f32[197]{0:T(256)S(1)} %broadcast_multiply_fusion.5) | copy-start | bytes 2368
  46.9 42.9 %copy-start.50 = (f32[197]{0:T(256)}, f32[197]{0:T(256)S(1)}, u32[]{:S(2)}) copy-start(f32[197]{0:T(256)S(1)} %add_rsqrt_fusion.1) | copy-start | bytes 2368
  47.2 42.7 %copy-start.21 = (f32[197,2,128]{2,1,0:T(2,128)}, f32[197,2,128]{2,1,0:T(2,128)S(1)}, u32[]{:S(2)}) copy-start(f32[197,2,128]{2,1,0:T(2,128)S(1)} %compare_convert_fusion) | copy-start | bytes 605188
  91.9 2.3 copy-start.8
  95.6 48.8 %copy-start.44 = (f32[768]{0:T(1024)S(1)}, f32[768]{0:T(1024)}, u32[]{:S(2)}) copy-start(f32[768]{0:T(1024)} %param.15) | copy-start | bytes 9220
  141.7 3.6 copy-start.34
  144.6 0.7 copy-start.6
  460.1 3.4 copy-start.24
  460.1 3.4 copy-start.26
  460.1 3.9 copy-start.36
  463.6 8.1 copy-start.28
  463.6 1.0 copy-start.20
  463.6 1.1 copy-start.22
  463.6 10.1 copy-start.5
  471.7 0.7 copy-start.17
  472.9 0.8 copy-start.23
  477.4 213.4 %reduce-scatter.12.cloned.1.call-start = ((), (), s32[]{:S(2)}) async-start(), calls=%async_computation.10 | async-start | bytes 5013504 | tf_op jit(solution)/shard_map/reduce_scatter | solution.py:207
  482.2 317.1 %reduce-scatter.10.cloned.1.call-start = ((), (), s32[]{:S(2)}) async-start(), calls=%async_computation.9 | async-start | bytes 5013504 | tf_op jit(solution)/shard_map/reduce_scatter | solution.py:199
  482.2 5.7 copy-start.15
  487.1 0.9 copy-start.12
  491.6 416.7 %reduce-scatter.8.cloned.1.call-start = ((), (), s32[]{:S(2)}) async-start(), calls=%async_computation.8 | async-start | bytes 5013504 | tf_op jit(solution)/shard_map/reduce_scatter | solution.py:199
  491.9 5.9 copy-start.16
  496.9 0.9 copy-start.14
  501.4 517.3 %reduce-scatter.6.cloned.1.call-start = ((), (), s32[]{:S(2)}) async-start(), calls=%async_computation.7 | async-start | bytes 5222400 | tf_op jit(solution)/shard_map/reduce_scatter | solution.py:235
  503.7 4.3 copy-start.13
  508.1 4.4 copy-start.35
  508.1 4.4 copy-start.49
  512.2 1.0 copy-start.25
  512.5 1.8 copy-start.7
  513.4 0.8 copy-start
  522.7 1.9 copy-start.11
  524.7 1.0 copy-start.10
  524.7 1.3 copy-start.1
  524.7 1.3 copy-start.4
  525.7 2.1 copy-start.39
  526.1 1.8 copy-start.41
  526.1 1.1 copy-start.9
  527.2 0.7 copy-start.51
  527.8 1.4 copy-start.37
  527.9 1.3 copy-start.30
  531.6 658.3 %all-reduce.5.cloned.1.call-start = ((), (), s32[]{:S(2)}) async-start(), calls=%async_computation.16 | async-start | bytes 2973696 | tf_op jit(solution)/shard_map/psum | solution.py:249
  692.6 326.1 %copy-start.38 = (bf16[12,64,197]{2,1,0:T(8,128)(2,1)S(1)}, bf16[12,64,197]{2,1,0:T(8,128)(2,1)}, u32[]{:S(2)}) copy-start(bf16[12,64,197]{2,1,0:T(8,128)(2,1)} %copy-done.37) | copy-start | bytes 907780
  692.6 326.1 %copy-start.40 = (bf16[12,64,197]{2,1,0:T(8,128)(2,1)S(1)}, bf16[12,64,197]{2,1,0:T(8,128)(2,1)}, u32[]{:S(2)}) copy-start(bf16[12,64,197]{2,1,0:T(8,128)(2,1)} %copy-done.39) | copy-start | bytes 907780
  692.6 326.1 %copy-start.42 = (bf16[12,64,197]{2,1,0:T(8,128)(2,1)S(1)}, bf16[12,64,197]{2,1,0:T(8,128)(2,1)}, u32[]{:S(2)}) copy-start(bf16[12,64,197]{2,1,0:T(8,128)(2,1)} %copy-done.41) | copy-start | bytes 907780
  1018.7 80.1 %copy-start.18 = (f32[197,2,128]{2,1,0:T(2,128)S(1)}, f32[197,2,128]{2,1,0:T(2,128)}, u32[]{:S(2)}) copy-start(f32[197,2,128]{2,1,0:T(2,128)} %copy-done.17) | copy-start | bytes 605188
  1018.7 80.1 %copy-start.27 = (bf16[1,128,768]{2,1,0:T(8,128)(2,1)S(1)}, bf16[1,128,768]{2,1,0:T(8,128)(2,1)}, u32[]{:S(2)}) copy-start(bf16[1,128,768]{2,1,0:T(8,128)(2,1)} %fusion.73) | copy-start | bytes 589828
  1018.8 80.1 %copy-start.29 = (bf16[1,128,768]{2,1,0:T(8,128)(2,1)S(1)}, bf16[1,128,768]{2,1,0:T(8,128)(2,1)}, u32[]{:S(2)}) copy-start(bf16[1,128,768]{2,1,0:T(8,128)(2,1)} %copy-done.28) | copy-start | bytes 589828
  1022.9 77.1 %copy-start.2 = (f32[197,768]{1,0:T(8,128)S(1)}, f32[197,768]{1,0:T(8,128)}, u32[]{:S(2)}) copy-start(f32[197,768]{1,0:T(8,128)} %copy-done) | copy-start | bytes 1815556
  1189.9 4.8 copy-start.32
  1189.9 5.9 copy-start.31
  (2 other events, 1.2 us)
Sparse Core Ops, SparseCore 0:
  10.7 76.0 all-gather.11
  89.5 52.1 all-gather.13
  145.0 76.9 all-gather.19
  224.6 76.5 all-gather.21
  304.3 76.5 all-gather.15
  383.5 76.5 all-gather.17
  477.5 103.9 reduce-scatter.13
  586.5 104.1 reduce-scatter.11
  695.1 104.1 reduce-scatter.9
  804.1 104.1 reduce-scatter.7
  912.8 105.8 reduce-scatter.5
  1022.5 167.3 all-reduce.4
where the time goes:
time: 1210 us; the launch traced here: 1200 us
  waiting for transfers between devices  951 us (79%)
  blocking collectives  106 us (9%)
  matrix products  81.6 us (7%)
  local copies, waits for them, and re-layouts  26.4 us (2%)
  other arithmetic  24 us (2%)
  between operations  15.4 us (1%)
    reduce_scatter x2, waiting for transfers between devices, body(): lax.psum_scatter(in_term(jnp.int32(0), shard_rows * lax.axis_size('shard'...  216 us
    reduce_scatter x2, waiting for transfers between devices, body(): lax.psum_scatter(out_term(jnp.int32(0), hid_rows * lax.axis_size('shard')...  159 us
    all_gather x2, waiting for transfers between devices, body(): lax.all_gather(w_expert_in[expert], 'shard', axis=0, tiled=True)  148 us
    all_gather x2, waiting for transfers between devices, body(): lax.all_gather(w_expert_out[expert], 'shard', axis=0, tiled=True)  143 us
    reduce_scatter x1, waiting for transfers between devices, body(): lax.psum_scatter(jnp.concatenate([jnp.einsum('rc,rk->ck', hidden1, grad_q...  108 us
    psum x1, waiting for transfers between devices, body(): lax.psum(dense_local, 'rep').astype(jnp.float32)  88.9 us
    psum x1, blocking collectives, body(): gain1_total, gain2_total = lax.psum((gain1, gain2), ('shard', 'rep'))  74.5 us
    all_gather x1, waiting for transfers between devices, body(): lax.all_gather(w_proj, 'shard', axis=0, tiled=True)  46.1 us
  transfers between devices with their start and end apart: 12, of which 12 were waited for; matrix products, arithmetic and copies ran while one was open for 9% of the time, Pallas kernels for 0%

commit v1 on v0

--- a/solution.py
+++ b/solution.py
@@ -245,8 +245,9 @@
         scatter_dimension=0,
         tiled=True,
     )
+    spread_the_pairs_all = lambda page: jnp.sum(jax.lax.all_gather(page, "rep"), axis=0)
     dense_total, in_total, out_total = (
-        lax.psum(dense_local, "rep").astype(jnp.float32),
+        spread_the_pairs_all(dense_local).astype(jnp.float32),
         lax.psum(jnp.stack(in_list).astype(jnp.bfloat16), "rep").astype(jnp.float32),
         lax.psum(jnp.stack(out_list).astype(jnp.bfloat16), "rep").astype(jnp.float32),
     )

time: 1210 us -> 1320 us (1.091)
  waiting for transfers between devices: 951 us -> 1060 us
    all_gather x0 -> x1, waiting for transfers between devices: none -> 113 us  [body(): jax.lax.all_gather(page, 'rep')]
  transfers between devices with their start and end apart: 12 -> 13, of which waited for: 12 -> 13; matrix products, arithmetic and copies ran while one was open for 9% -> 8% of each run, Pallas kernels for 0% -> 0%
where the time goes in v1:
time: 1320 us; the launch traced here: 1310 us
  waiting for transfers between devices  1060 us (80%)
  blocking collectives  105 us (8%)
  matrix products  81.8 us (6%)
  other arithmetic  28.3 us (2%)
  local copies, waits for them, and re-layouts  23.7 us (2%)
  between operations  15 us (1%)
    reduce_scatter x2, waiting for transfers between devices, body(): lax.psum_scatter(in_term(jnp.int32(0), shard_rows * lax.axis_size('shard'...  216 us
    reduce_scatter x2, waiting for transfers between devices, body(): lax.psum_scatter(out_term(jnp.int32(0), hid_rows * lax.axis_size('shard')...  159 us
    all_gather x2, waiting for transfers between devices, body(): lax.all_gather(w_expert_in[expert], 'shard', axis=0, tiled=True)  148 us
    all_gather x2, waiting for transfers between devices, body(): lax.all_gather(w_expert_out[expert], 'shard', axis=0, tiled=True)  143 us
    all_gather x1, waiting for transfers between devices, body(): jax.lax.all_gather(page, 'rep')  113 us
    reduce_scatter x1, waiting for transfers between devices, body(): lax.psum_scatter(jnp.concatenate([jnp.einsum('rc,rk->ck', hidden1, grad_q...  108 us
    psum x1, waiting for transfers between devices, body(): lax.psum(jnp.stack(in_list).astype(jnp.bfloat16), 'rep').astype(jnp.float32)  84.8 us
    psum x1, blocking collectives, body(): gain1_total, gain2_total = lax.psum((gain1, gain2), ('shard', 'rep'))  74.4 us
  transfers between devices with their start and end apart: 13, of which 13 were waited for; matrix products, arithmetic and copies ran while one was open for 8% of the time, Pallas kernels for 0%

profile of v1, /device:TPU:24, one launch (start us, length us, event | category | flops | bytes accessed | tf_op | source)
XLA Modules:
  0.0 1313.7 jit_solution(9555919561906572955)
XLA Ops:
  8.7 1.9 fusion.130
  10.7 0.9 fusion.129
  14.3 31.0 %all-gather.5 = bf16[16,48,32]{1,2,0:T(8,128)(2,1)S(1)} all-gather(bf16[1,48,32]{1,2,0:T(8,128)(2,1)S(1)} %bitcast.201), channel_id=1, replica_groups=mesh['shard'=16,'rep'=16] {'shard'}, dimensions={0}, use_global_device_ids=true | all-gather | bytes 52224 | tf_op jit(solution)/shard_map/all_gather | solution.py:124
  45.4 0.8 reshape.248
  47.8 39.1 %all-gather.14.cloned.1.call-done = bf16[768,2304]{1,0:T(8,128)(2,1)} async-done(((bf16[48,2304]{1,0:T(8,128)(2,1)}), bf16[768,2304]{1,0:T(8,128)(2,1)}) %all-gather.14.cloned.1.call-update) | async-done | bytes 3538960 | tf_op jit(solution)/shard_map/all_gather | solution.py:122
  86.8 3.0 convolution_convert_fusion.5
  89.9 0.9 copy.110
  90.8 0.9 copy.109
  91.9 1.8 multiply_reduce_fusion
  94.3 1.4 convolution_convert_fusion.10
  95.6 46.1 %all-gather.16.cloned.1.call-done = bf16[768,768]{1,0:T(8,128)(2,1)} async-done(((bf16[48,768]{1,0:T(8,128)(2,1)}), bf16[768,768]{1,0:T(8,128)(2,1)}) %all-gather.16.cloned.1.call-update) | async-done | bytes 1179664 | tf_op jit(solution)/shard_map/all_gather | solution.py:123
  141.7 1.9 fusion.131
  144.6 0.7 copy-done.6
  146.3 1.4 copy.115
  147.7 2.0 convolution_convert_fusion.9
  149.7 72.3 %all-gather.22.cloned.1.call-done = bf16[1,768,3072]{2,1,0:T(8,128)(2,1)} async-done(((bf16[1,48,3072]{2,1,0:T(8,128)(2,1)}), bf16[1,768,3072]{2,1,0:T(8,128)(2,1)}) %all-gather.22.cloned.1.call-update) | async-done | bytes 4718608 | tf_op jit(solution)/shard_map/all_gather | solution.py:149
  222.0 7.7 fusion.34
  229.7 71.5 %all-gather.24.cloned.1.call-done = bf16[1,3072,768]{2,1,0:T(8,128)(2,1)} async-done(((bf16[1,192,768]{2,1,0:T(8,128)(2,1)}), bf16[1,3072,768]{2,1,0:T(8,128)(2,1)}) %all-gather.24.cloned.1.call-update) | async-done | bytes 4718608 | tf_op jit(solution)/shard_map/all_gather | solution.py:150
  301.2 4.0 fusion.73
  305.2 75.7 %all-gather.18.cloned.1.call-done = bf16[1,768,3072]{2,1,0:T(8,128)(2,1)} async-done(((bf16[1,48,3072]{2,1,0:T(8,128)(2,1)}), bf16[1,768,3072]{2,1,0:T(8,128)(2,1)}) %all-gather.18.cloned.1.call-update) | async-done | bytes 4718608 | tf_op jit(solution)/shard_map/all_gather | solution.py:149
  380.9 8.1 fusion.31
  389.1 71.0 %all-gather.20.cloned.1.call-done = bf16[1,3072,768]{2,1,0:T(8,128)(2,1)} async-done(((bf16[1,192,768]{2,1,0:T(8,128)(2,1)}), bf16[1,3072,768]{2,1,0:T(8,128)(2,1)}) %all-gather.20.cloned.1.call-update) | async-done | bytes 4718608 | tf_op jit(solution)/shard_map/all_gather | solution.py:150
  460.1 3.4 fusion.79
  464.7 7.0 fusion.100
  472.9 0.7 copy-done.23
  473.7 3.7 convolution_convert_fusion
  477.4 4.8 convolution_convert_fusion.1
  482.3 4.8 fusion.22
  487.1 0.9 copy-done.12
  488.0 3.6 convolution_convert_fusion.2
  491.9 5.0 fusion.25
  496.9 0.9 copy-done.14
  497.7 3.5 convolution_convert_fusion.3
  501.3 1.6 copy.121
  502.9 0.7 select_reduce_fusion
  503.6 4.3 fusion.82
  508.0 4.1 fusion.76
  513.3 0.8 copy-done
  514.1 1.3 convolution_convert_fusion.11
  515.4 1.9 copy.122
  517.3 2.0 copy.123
  519.3 1.1 convolution_convert_fusion.12
  520.5 0.8 copy.129
  521.3 1.4 multiply_reduce_fusion.1
  522.7 1.9 multiply_convert_fusion
  527.8 1.3 convolution_convert_fusion.4
  529.1 2.4 pad_maximum_fusion
  531.6 49.9 %reduce-scatter.14.cloned.1.call-done = bf16[192,768]{1,0:T(8,128)(2,1)} async-done(((bf16[3072,768]{1,0:T(8,128)(2,1)}), bf16[192,768]{1,0:T(8,128)(2,1)}) %reduce-scatter.14.cloned.1.call-update) | async-done | bytes 294928 | tf_op jit(solution)/shard_map/reduce_scatter | solution.py:207
  581.5 109.2 %reduce-scatter.12.cloned.1.call-done = bf16[192,768]{1,0:T(8,128)(2,1)} async-done(((bf16[3072,768]{1,0:T(8,128)(2,1)}), bf16[192,768]{1,0:T(8,128)(2,1)}) %reduce-scatter.12.cloned.1.call-update) | async-done | bytes 294928 | tf_op jit(solution)/shard_map/reduce_scatter | solution.py:207
  690.7 1.9 pad_maximum_fusion.3
  692.6 106.6 %reduce-scatter.10.cloned.1.call-done = bf16[48,3072]{1,0:T(8,128)(2,1)} async-done(((bf16[768,3072]{1,0:T(8,128)(2,1)}), bf16[48,3072]{1,0:T(8,128)(2,1)}) %reduce-scatter.10.cloned.1.call-update) | async-done | bytes 294928 | tf_op jit(solution)/shard_map/reduce_scatter | solution.py:199
  799.2 109.0 %reduce-scatter.8.cloned.1.call-done = bf16[48,3072]{1,0:T(8,128)(2,1)} async-done(((bf16[768,3072]{1,0:T(8,128)(2,1)}), bf16[48,3072]{1,0:T(8,128)(2,1)}) %reduce-scatter.8.cloned.1.call-update) | async-done | bytes 294928 | tf_op jit(solution)/shard_map/reduce_scatter | solution.py:199
  908.2 1.9 pad_maximum_fusion.2
  910.2 108.3 %reduce-scatter.6.cloned.1.call-done = bf16[48,3104]{1,0:T(8,128)(2,1)} async-done(((bf16[768,3104]{1,0:T(8,128)(2,1)}), bf16[48,3104]{1,0:T(8,128)(2,1)}) %reduce-scatter.6.cloned.1.call-update) | async-done | bytes 298000 | tf_op jit(solution)/shard_map/reduce_scatter | solution.py:235
  1018.6 4.2 fusion.96
  1022.8 74.4 %all-reduce.1 = (f32[768]{0:T(1024)}, f32[768]{0:T(1024)}) all-reduce(f32[768]{0:T(1024)S(1)} %get-tuple-element.56, f32[768]{0:T(1024)S(1)} %get-tuple-element.54), channel_id=1, replica_groups=mesh['shard'=16,'rep'=16] {'shard','rep'}, use_global_device_ids=true, to_apply=%region_24.25 | all-reduce | flops 1536 | bytes 12288 | tf_op jit(solution)/shard_map/psum | solution.py:234
  1098.5 1.1 fusion.60
  1099.6 1.1 fusion.95
  1100.7 84.8 %all-reduce.5.cloned.1.call-done = (bf16[2,48,3072]{2,1,0:T(8,128)(2,1)}, bf16[2,192,768]{2,1,0:T(8,128)(2,1)}) async-done(((bf16[2,48,3072]{2,1,0:T(8,128)(2,1)}, bf16[2,192,768]{2,1,0:T(8,128)(2,1)}), (bf16[2,48,3072]{2,1,0:T(8,128)(2,1)}, bf16[2,192,768]{2,1,0:T(8,128)(2,1)})) %all-reduce.5.cloned.1.call-update) | async-done | bytes 1179664 | tf_op jit(solution)/shard_map/psum | solution.py:251
  1185.5 2.2 convert_element_type.193
  1187.7 1.1 convert_element_type.196
  1188.8 112.8 %all-gather.26.cloned.1.call-done = bf16[768,3104]{1,0:T(8,128)(2,1)} async-done(((bf16[48,3104]{1,0:T(8,128)(2,1)}), bf16[768,3104]{1,0:T(8,128)(2,1)}) %all-gather.26.cloned.1.call-update) | async-done | bytes 4767760 | tf_op jit(solution)/shard_map/all_gather | solution.py:248
  1301.6 3.2 reduce_sum.224
  1305.5 0.8 slice.84
  (181 shorter events, 18.3 us)
Async XLA Ops:
  7.2 3.5 copy-start.32
  7.2 79.7 %all-gather.14.cloned.1.call-start = ((), (), s32[]{:S(2)}) async-start(), calls=%async_computation.5 | async-start | bytes 3760128 | tf_op jit(solution)/shard_map/all_gather | solution.py:122
  7.9 133.8 %all-gather.16.cloned.1.call-start = ((), (), s32[]{:S(2)}) async-start(), calls=%async_computation.6 | async-start | bytes 1253376 | tf_op jit(solution)/shard_map/all_gather | solution.py:123
  8.7 4.2 copy-start.42
  8.7 213.3 %all-gather.22.cloned.1.call-start = ((), (), s32[]{:S(2)}) async-start(), calls=%async_computation.14 | async-start | bytes 5013504 | tf_op jit(solution)/shard_map/all_gather | solution.py:149
  10.6 3.7 copy-start.51
  10.6 35.6 %copy-start.52 = (s32[2]{0:T(128)S(1)}, s32[2]{0:T(128)}, u32[]{:S(2)}) copy-start(s32[2]{0:T(128)} %param.20) | copy-start | bytes 28
  10.7 35.8 %copy-start.3 = (bf16[197,768]{1,0:T(8,128)(2,1)S(1)}, bf16[197,768]{1,0:T(8,128)(2,1)}, u32[]{:S(2)}) copy-start(bf16[197,768]{1,0:T(8,128)(2,1)} %param.11) | copy-start | bytes 907780
  10.7 290.5 %all-gather.24.cloned.1.call-start = ((), (), s32[]{:S(2)}) async-start(), calls=%async_computation.15 | async-start | bytes 5013504 | tf_op jit(solution)/shard_map/all_gather | solution.py:150
  11.6 75.2 %copy-start.44 = (f32[768]{0:T(1024)S(1)}, f32[768]{0:T(1024)}, u32[]{:S(2)}) copy-start(f32[768]{0:T(1024)} %param.12) | copy-start | bytes 9220
  11.6 369.3 %all-gather.18.cloned.1.call-start = ((), (), s32[]{:S(2)}) async-start(), calls=%async_computation.12 | async-start | bytes 5013504 | tf_op jit(solution)/shard_map/all_gather | solution.py:149
  12.2 447.9 %all-gather.20.cloned.1.call-start = ((), (), s32[]{:S(2)}) async-start(), calls=%async_computation.13 | async-start | bytes 5013504 | tf_op jit(solution)/shard_map/all_gather | solution.py:150
  12.8 568.8 %reduce-scatter.14.cloned.1.call-start = ((), (), s32[]{:S(2)}) async-start(), calls=%async_computation.11 | async-start | bytes 5013504 | tf_op jit(solution)/shard_map/reduce_scatter | solution.py:207
  46.5 43.3 %copy-start.19 = (f32[197,2,2]{2,1,0:T(2,128)}, f32[197,2,2]{2,1,0:T(2,128)S(1)}, u32[]{:S(2)}) copy-start(f32[197,2,2]{2,1,0:T(2,128)S(1)} %copy.112) | copy-start | bytes 9460
  46.6 43.2 %copy-start.45 = (f32[197]{0:T(256)}, f32[197]{0:T(256)S(1)}, u32[]{:S(2)}) copy-start(f32[197]{0:T(256)S(1)} %broadcast_multiply_fusion.5) | copy-start | bytes 2368
  46.9 42.9 %copy-start.49 = (f32[197]{0:T(256)}, f32[197]{0:T(256)S(1)}, u32[]{:S(2)}) copy-start(f32[197]{0:T(256)S(1)} %add_rsqrt_fusion.1) | copy-start | bytes 2368
  47.2 42.7 %copy-start.21 = (f32[197,2,128]{2,1,0:T(2,128)}, f32[197,2,128]{2,1,0:T(2,128)S(1)}, u32[]{:S(2)}) copy-start(f32[197,2,128]{2,1,0:T(2,128)S(1)} %compare_convert_fusion) | copy-start | bytes 605188
  91.9 2.3 copy-start.8
  95.6 48.8 %copy-start.43 = (f32[768]{0:T(1024)S(1)}, f32[768]{0:T(1024)}, u32[]{:S(2)}) copy-start(f32[768]{0:T(1024)} %param.15) | copy-start | bytes 9220
  141.7 3.6 copy-start.33
  144.6 0.7 copy-start.6
  460.1 3.4 copy-start.24
  460.1 3.4 copy-start.26
  460.1 3.9 copy-start.35
  463.6 8.1 copy-start.28
  463.6 1.0 copy-start.20
  463.6 1.1 copy-start.22
  463.6 10.1 copy-start.5
  471.7 0.7 copy-start.17
  472.9 0.8 copy-start.23
  477.4 213.3 %reduce-scatter.12.cloned.1.call-start = ((), (), s32[]{:S(2)}) async-start(), calls=%async_computation.10 | async-start | bytes 5013504 | tf_op jit(solution)/shard_map/reduce_scatter | solution.py:207
  482.2 317.0 %reduce-scatter.10.cloned.1.call-start = ((), (), s32[]{:S(2)}) async-start(), calls=%async_computation.9 | async-start | bytes 5013504 | tf_op jit(solution)/shard_map/reduce_scatter | solution.py:199
  482.3 5.7 copy-start.15
  487.1 0.9 copy-start.12
  491.6 416.6 %reduce-scatter.8.cloned.1.call-start = ((), (), s32[]{:S(2)}) async-start(), calls=%async_computation.8 | async-start | bytes 5013504 | tf_op jit(solution)/shard_map/reduce_scatter | solution.py:199
  491.9 5.9 copy-start.16
  496.8 0.9 copy-start.14
  501.3 517.2 %reduce-scatter.6.cloned.1.call-start = ((), (), s32[]{:S(2)}) async-start(), calls=%async_computation.7 | async-start | bytes 5222400 | tf_op jit(solution)/shard_map/reduce_scatter | solution.py:235
  503.6 4.3 copy-start.13
  508.0 4.4 copy-start.34
  508.0 4.4 copy-start.48
  512.1 1.0 copy-start.25
  512.4 1.8 copy-start.7
  513.3 0.8 copy-start
  522.6 1.9 copy-start.11
  524.6 1.0 copy-start.10
  524.6 1.3 copy-start.1
  524.6 1.3 copy-start.4
  525.6 2.1 copy-start.38
  526.0 1.8 copy-start.40
  526.0 1.1 copy-start.9
  527.1 0.7 copy-start.50
  527.7 1.4 copy-start.36
  527.8 1.3 copy-start.30
  531.5 654.0 %all-reduce.5.cloned.1.call-start = ((), (), s32[]{:S(2)}) async-start(), calls=%async_computation.17 | async-start | bytes 2359296 | tf_op jit(solution)/shard_map/psum | solution.py:251
  692.6 325.9 %copy-start.37 = (bf16[12,64,197]{2,1,0:T(8,128)(2,1)S(1)}, bf16[12,64,197]{2,1,0:T(8,128)(2,1)}, u32[]{:S(2)}) copy-start(bf16[12,64,197]{2,1,0:T(8,128)(2,1)} %copy-done.36) | copy-start | bytes 907780
  692.6 325.9 %copy-start.39 = (bf16[12,64,197]{2,1,0:T(8,128)(2,1)S(1)}, bf16[12,64,197]{2,1,0:T(8,128)(2,1)}, u32[]{:S(2)}) copy-start(bf16[12,64,197]{2,1,0:T(8,128)(2,1)} %copy-done.38) | copy-start | bytes 907780
  692.6 325.9 %copy-start.41 = (bf16[12,64,197]{2,1,0:T(8,128)(2,1)S(1)}, bf16[12,64,197]{2,1,0:T(8,128)(2,1)}, u32[]{:S(2)}) copy-start(bf16[12,64,197]{2,1,0:T(8,128)(2,1)} %copy-done.40) | copy-start | bytes 907780
  910.1 391.4 %all-gather.26.cloned.1.call-start = ((), (), s32[]{:S(2)}) async-start(), calls=%async_computation.16 | async-start | bytes 5222400 | tf_op jit(solution)/shard_map/all_gather | solution.py:248
  1018.6 79.9 %copy-start.18 = (f32[197,2,128]{2,1,0:T(2,128)S(1)}, f32[197,2,128]{2,1,0:T(2,128)}, u32[]{:S(2)}) copy-start(f32[197,2,128]{2,1,0:T(2,128)} %copy-done.17) | copy-start | bytes 605188
  1018.6 79.9 %copy-start.27 = (bf16[1,128,768]{2,1,0:T(8,128)(2,1)S(1)}, bf16[1,128,768]{2,1,0:T(8,128)(2,1)}, u32[]{:S(2)}) copy-start(bf16[1,128,768]{2,1,0:T(8,128)(2,1)} %fusion.73) | copy-start | bytes 589828
  1018.6 79.9 %copy-start.29 = (bf16[1,128,768]{2,1,0:T(8,128)(2,1)S(1)}, bf16[1,128,768]{2,1,0:T(8,128)(2,1)}, u32[]{:S(2)}) copy-start(bf16[1,128,768]{2,1,0:T(8,128)(2,1)} %copy-done.28) | copy-start | bytes 589828
  1022.8 76.9 %copy-start.2 = (f32[197,768]{1,0:T(8,128)S(1)}, f32[197,768]{1,0:T(8,128)}, u32[]{:S(2)}) copy-start(f32[197,768]{1,0:T(8,128)} %copy-done) | copy-start | bytes 1815556
  1185.5 2.2 copy-start.31
  (2 other events, 1.2 us)
Sparse Core Ops, SparseCore 0:
  10.7 76.0 all-gather.13
  89.5 52.1 all-gather.15
  145.0 76.9 all-gather.21
  224.6 76.5 all-gather.23
  304.3 76.5 all-gather.17
  383.5 76.5 all-gather.19
  477.5 103.9 reduce-scatter.13
  586.5 104.1 reduce-scatter.11
  695.1 104.0 reduce-scatter.9
  804.0 104.1 reduce-scatter.7
  912.7 105.7 reduce-scatter.5
  1022.2 163.2 all-reduce.4
  1187.3 114.2 all-gather.25
